TPU v7x, 512 devices: a whole 4x4x16 slice. The times are simulated.
512 devices in a mesh: line: 8 (over y_hi, x), bus: 32 (over y_lo, z), scen: 2 (over core).
Axes of the slice: x: 4, y: 4 (y_hi: 2, y_lo: 2; y = y_hi * 2 + y_lo), z: 16, core: 2. Of those that a mesh axis runs over, the one named last changes fastest.
Arguments:
- ptdf: bfloat16 [8192, 49152], P('line', 'bus'), may hold values from -0.0546875 to 0.0546875
- injections: bfloat16 [49152, 512], P('bus', 'scen'), may hold values from -6 to 6
- lodf: bfloat16 [8192, 2048], P(('line', 'bus')), may hold values from -3 to 3
- ratings: float32 [8192], P(('line', 'bus')), may hold values from 0.5 to 2
- outages: int32 [2048], replicated, may hold values from 0 to 8191, as said below
Outputs:
- overload: float32 [8192, 2048], P(('line', 'bus'))
Inputs may be any that keep to these rules, and one draw needn't show every extreme that they name: `outages`: 2048 distinct line indices.
All inputs are finite; a program needn't handle non-finite values.
Results may differ from a plain program's by a relative error of at most 0.0003.
Values sent between devices are 32-bit elements; how exact they have to be, the bound alone decides.
No kernel may reach another device: no remote copies, remote signals or barrier semaphores. Data moves between devices by JAX's collectives and lax.ppermute only.
A program may use at most 64 MiB of HBM per device.

v0:
```python
import jax
import jax.numpy as jnp
from jax import lax
from jax.sharding import PartitionSpec as P

softness = 0.2


def base_flow_term(base_rows, lodf_rows, outage_flow):
    return (
        base_rows[:, None, :] + lodf_rows.astype(jnp.float32)[:, :, None] * outage_flow[None, :, :]
    )


def overload_sum(base_flow, outage_flow, lodf, ratings):
    lines_here = base_flow.shape[0]
    groups = lines_here // 4

    def line_block(pieces):
        base_rows, lodf_rows, rating_rows = pieces
        post_flow = base_flow_term(base_rows, lodf_rows, outage_flow)
        margin = (jnp.abs(post_flow) - rating_rows[:, None, None]) / (
            softness * rating_rows[:, None, None]
        )
        return jnp.sum(jax.nn.sigmoid(margin), axis=2)

    summed = lax.map(
        line_block,
        (base_flow.reshape(groups, 4, -1), lodf.reshape(groups, 4, -1), ratings.reshape(groups, 4)),
    )
    return summed.reshape(lines_here, -1)


def select_rows(flows, outages, first):
    count = flows.shape[0]
    offset = outages - first
    inside = (offset >= 0) & (offset < count)
    picked = jnp.take(flows, jnp.clip(offset, 0, count - 1), axis=0)
    return jnp.where(inside[:, None], picked, 0.0)


def shards(ptdf, injections, lodf, ratings, outages):
    own_rows = lodf.shape[0]
    base_flow = lax.psum_scatter(
        jnp.dot(ptdf, injections, preferred_element_type=jnp.float32),
        "bus",
        scatter_dimension=0,
        tiled=True,
    )
    first_own = (lax.axis_index("line") * lax.axis_size("bus") + lax.axis_index("bus")) * own_rows
    outage_flow = lax.psum(select_rows(base_flow, outages, first_own), ("line", "bus"))
    local_sum = overload_sum(base_flow, outage_flow, lodf, ratings)
    total = lax.psum(local_sum, "scen")
    return total / (injections.shape[1] * lax.axis_size("scen"))


def solution(mesh):
    return jax.shard_map(
        shards,
        mesh=mesh,
        in_specs=(
            P("line", "bus"),
            P("bus", "scen"),
            P(("line", "bus"), None),
            P(("line", "bus")),
            P(),
        ),
        out_specs=P(("line", "bus"), None),
        check_vma=False,
    )
```

profile of v0, /device:TPU:1, one launch (start us, length us, event | category | flops | bytes accessed | tf_op | source)
XLA Modules:
  0.0 666.5 jit_solution(12721925452298086936)
XLA Ops:
  6.5 0.0 copy-start
  6.5 0.0 copy-start.3
  6.5 0.0 reduce-scatter.2.cloned.1.call-start
  6.5 1.9 copy-done
  8.4 3.1 fusion.4
  11.5 0.0 reduce-scatter.2.cloned.1.call-update
  11.5 0.0 all-reduce.3.cloned.1.call-start
  11.6 0.0 copy-done.3
  11.6 118.5 %reduce-scatter.2.cloned.1.call-done = f32[32,256]{1,0:T(8,128)} async-done(((f32[1024,256]{1,0:T(8,128)}), f32[32,256]{1,0:T(8,128)}) %reduce-scatter.2.cloned.1.call-update) | async-done | bytes 32784 | tf_op jit(solution)/shard_map/reduce_scatter | solution.py:44
  130.1 9.3 %gather_fusion = f32[2048,256]{1,0:T(8,128)} fusion(f32[32,256]{1,0:T(8,128)} %reduce-scatter.2.cloned.1.call-done, s32[2048]{0:T(1024)S(1)} %fusion.2), kind=kCustom, calls=%fused_computation | custom fusion | bytes 4202496 | tf_op jit(solution)/shard_map/jit(_take)/gather | solution.py:38
  139.4 0.0 copy-start.2
  139.4 0.0 copy-start.4
  139.4 0.0 copy-start.1
  139.4 4.3 select_select_fusion
  143.8 0.0 all-reduce.3.cloned.1.call-update
  143.8 0.0 all-reduce.5.cloned.1.call-start
  143.9 0.0 copy-done.2
  143.9 0.1 reshape.38
  143.9 0.0 copy-done.4
  143.9 0.1 reshape.39
  144.0 0.0 copy-done.1
  144.0 420.5 %all-reduce.3.cloned.1.call-done = f32[2048,256]{1,0:T(8,128)} async-done(((f32[2048,256]{1,0:T(8,128)}), f32[2048,256]{1,0:T(8,128)}) %all-reduce.3.cloned.1.call-update) | async-done | bytes 2097168 | tf_op jit(solution)/shard_map/psum | solution.py:51
  564.5 46.5 %while.10 = (s32[]{:T(128)}, f32[8,4,2048]{2,1,0:T(4,128)}, f32[8,4,256]{2,1,0:T(4,128)S(1)}, bf16[8,4,2048]{2,1,0:T(4,128)(2,1)S(1)}, f32[2048,256]{1,0:T(8,128)}, /*index=5*/f32[8,4]{1,0:T(8,128)S(1)}, s32[]{:T(128)}) while((s32[]{:T(128)}, f32[8,4,2048]{2,1,0:T(4,128)}, f32[8,4,256]{2,1,0:T(4,128)S(1)}, bf16[8,4,2048]{2,1,0:T(4,128)(2,1)S(1)}, ...), condition=%wide.region_4.5_spmd, body=%wide.region_2.4_spmd.sunk | while | flops 18874372 | bytes 2290345 | solution.py:27
  564.5 5.1 fusion.8
  569.7 0.6 bitcast_dynamic-update-slice_fusion.2
  570.4 5.1 fusion.8
  575.5 0.6 bitcast_dynamic-update-slice_fusion.2
  576.2 5.1 fusion.8
  581.3 0.6 bitcast_dynamic-update-slice_fusion.2
  582.0 5.1 fusion.8
  587.1 0.6 bitcast_dynamic-update-slice_fusion.2
  587.8 5.1 fusion.8
  592.9 0.6 bitcast_dynamic-update-slice_fusion.2
  593.6 5.1 fusion.8
  598.7 0.6 bitcast_dynamic-update-slice_fusion.2
  599.4 5.1 fusion.8
  604.5 0.6 bitcast_dynamic-update-slice_fusion.2
  605.2 5.1 fusion.8
  610.4 0.6 bitcast_dynamic-update-slice_fusion.2
  611.0 1.7 reshape.40
  612.7 0.0 all-reduce.5.cloned.1.call-update
  612.7 45.5 %all-reduce.5.cloned.1.call-done = f32[32,2048]{1,0:T(8,128)} async-done(((f32[32,2048]{1,0:T(8,128)}), f32[32,2048]{1,0:T(8,128)}) %all-reduce.5.cloned.1.call-update) | async-done | bytes 262160 | tf_op jit(solution)/shard_map/psum | solution.py:53
  658.3 1.7 broadcast_multiply_fusion.1
  (28 shorter events, 0.2 us)
Async XLA Ops:
  6.5 1.9 copy-start
  6.5 5.1 copy-start.3
  6.5 123.6 %reduce-scatter.2.cloned.1.call-start = ((), (), s32[]{:S(2)}) async-start(), calls=%async_computation.1 | async-start | bytes 1081344 | tf_op jit(solution)/shard_map/reduce_scatter | solution.py:44
  11.5 553.0 %all-reduce.3.cloned.1.call-start = ((), (), s32[]{:S(2)}) async-start(), calls=%async_computation.2 | async-start | bytes 4194304 | tf_op jit(solution)/shard_map/psum | solution.py:51
  139.4 4.4 copy-start.2
  139.4 4.5 copy-start.4
  139.4 4.6 copy-start.1
  143.8 514.5 %all-reduce.5.cloned.1.call-start = ((), (), s32[]{:S(2)}) async-start(), calls=%async_computation.3 | async-start | bytes 524288 | tf_op jit(solution)/shard_map/psum | solution.py:53
Sparse Core Ops, SparseCore 0:
  11.7 118.4 reduce-scatter.1
  143.9 420.5 all-reduce.2
  612.9 45.3 all-reduce.4
where the time goes:
time: 667 us; the launch traced here: 666 us
  waiting for transfers between devices  585 us (88%)
  other arithmetic  47.3 us (7%)
  local copies, waits for them, and re-layouts  18.2 us (3%)
  between operations  13.2 us (2%)
    psum x1, waiting for transfers between devices, shards(): lax.psum(select_rows(base_flow, outages, first_own), ('line', 'bus'))  420 us
    reduce_scatter x1, waiting for transfers between devices, shards(): lax.psum_scatter(jnp.dot(ptdf, injections, preferred_element_type=jnp.flo...  118 us
    psum x1, waiting for transfers between devices, shards(): total = lax.psum(local_sum, 'scen')  45.5 us
    reduce_sum x8, other arithmetic, line_block(): return jnp.sum(jax.nn.sigmoid(margin), axis=2)  41.2 us
  transfers between devices with their start and end apart: 3, of which 3 were waited for; matrix products, arithmetic and copies ran while one was open for 0% of the time, Pallas kernels for 0%

commit v1 on v0

--- a/solution.py
+++ b/solution.py
@@ -48,7 +48,7 @@
         tiled=True,
     )
     first_own = (lax.axis_index("line") * lax.axis_size("bus") + lax.axis_index("bus")) * own_rows
-    outage_flow = lax.psum(select_rows(base_flow, outages, first_own), ("line", "bus"))
+    outage_flow = lax.psum(lax.psum(select_rows(base_flow, outages, first_own), "bus"), "line")
     local_sum = overload_sum(base_flow, outage_flow, lodf, ratings)
     total = lax.psum(local_sum, "scen")
     return total / (injections.shape[1] * lax.axis_size("scen"))

time: 667 us -> 625 us (0.937)
  waiting for transfers between devices: 585 us -> 542 us
    psum x1 -> x2, waiting for transfers between devices: 420 us -> 379 us  [the longest x1 258 us: shards(): lax.psum(select_rows(base_flow, outages, first_own), 'bus')]
  transfers between devices with their start and end apart: 3 -> 4, of which waited for: 3 -> 4; matrix products, arithmetic and copies ran while one was open for 0% -> 0% of each run, Pallas kernels for 0% -> 0%
where the time goes in v1:
time: 625 us; the launch traced here: 624 us
  waiting for transfers between devices  542 us (87%)
  other arithmetic  47.3 us (8%)
  local copies, waits for them, and re-layouts  18.2 us (3%)
  between operations  13.2 us (2%)
    psum x1, waiting for transfers between devices, shards(): lax.psum(select_rows(base_flow, outages, first_own), 'bus')  258 us
    psum x1, waiting for transfers between devices, shards(): lax.psum(lax.psum(select_rows(base_flow, outages, first_own), 'bus'), 'li...  121 us
    reduce_scatter x1, waiting for transfers between devices, shards(): lax.psum_scatter(jnp.dot(ptdf, injections, preferred_element_type=jnp.flo...  118 us
    psum x1, waiting for transfers between devices, shards(): total = lax.psum(local_sum, 'scen')  44.5 us
    reduce_sum x8, other arithmetic, line_block(): return jnp.sum(jax.nn.sigmoid(margin), axis=2)  41.3 us
  transfers between devices with their start and end apart: 4, of which 4 were waited for; matrix products, arithmetic and copies ran while one was open for 0% of the time, Pallas kernels for 0%

profile of v1, /device:TPU:1, one launch (start us, length us, event | category | flops | bytes accessed | tf_op | source)
XLA Modules:
  0.0 624.1 jit_solution(15307541530949354076)
XLA Ops:
  6.5 0.0 copy-start
  6.5 0.0 copy-start.3
  6.5 0.0 reduce-scatter.2.cloned.1.call-start
  6.5 1.9 copy-done
  8.4 3.1 fusion.4
  11.5 0.0 reduce-scatter.2.cloned.1.call-update
  11.5 0.0 all-reduce.4.cloned.1.call-start
  11.6 0.0 copy-done.3
  11.6 118.5 %reduce-scatter.2.cloned.1.call-done = f32[32,256]{1,0:T(8,128)} async-done(((f32[1024,256]{1,0:T(8,128)}), f32[32,256]{1,0:T(8,128)}) %reduce-scatter.2.cloned.1.call-update) | async-done | bytes 32784 | tf_op jit(solution)/shard_map/reduce_scatter | solution.py:44
  130.1 9.3 %gather_fusion = f32[2048,256]{1,0:T(8,128)} fusion(f32[32,256]{1,0:T(8,128)} %reduce-scatter.2.cloned.1.call-done, s32[2048]{0:T(1024)S(1)} %fusion.2), kind=kCustom, calls=%fused_computation | custom fusion | bytes 4202496 | tf_op jit(solution)/shard_map/jit(_take)/gather | solution.py:38
  139.4 4.3 select_select_fusion
  143.7 0.0 copy-start.2
  143.7 0.0 copy-start.4
  143.7 0.0 copy-start.1
  143.7 0.0 all-reduce.4.cloned.1.call-update
  143.8 0.0 all-reduce.6.cloned.1.call-start
  143.8 257.9 %all-reduce.4.cloned.1.call-done = f32[2048,256]{1,0:T(8,128)} async-done(((f32[2048,256]{1,0:T(8,128)}), f32[2048,256]{1,0:T(8,128)}) %all-reduce.4.cloned.1.call-update) | async-done | bytes 2097168 | tf_op jit(solution)/shard_map/psum | solution.py:51
  401.7 0.0 all-reduce.6.cloned.1.call-update
  401.8 0.0 all-reduce.8.cloned.1.call-start
  401.8 0.0 copy-done.2
  401.8 0.1 reshape.38
  401.9 0.0 copy-done.4
  401.9 0.1 reshape.39
  402.0 0.0 copy-done.1
  402.0 121.1 %all-reduce.6.cloned.1.call-done = f32[2048,256]{1,0:T(8,128)} async-done(((f32[2048,256]{1,0:T(8,128)}), f32[2048,256]{1,0:T(8,128)}) %all-reduce.6.cloned.1.call-update) | async-done | bytes 2097168 | tf_op jit(solution)/shard_map/psum | solution.py:51
  523.1 46.6 %while.10 = (s32[]{:T(128)}, f32[8,4,2048]{2,1,0:T(4,128)}, f32[8,4,256]{2,1,0:T(4,128)S(1)}, bf16[8,4,2048]{2,1,0:T(4,128)(2,1)S(1)}, f32[2048,256]{1,0:T(8,128)}, /*index=5*/f32[8,4]{1,0:T(8,128)S(1)}, s32[]{:T(128)}) while((s32[]{:T(128)}, f32[8,4,2048]{2,1,0:T(4,128)}, f32[8,4,256]{2,1,0:T(4,128)S(1)}, bf16[8,4,2048]{2,1,0:T(4,128)(2,1)S(1)}, ...), condition=%wide.region_5.6_spmd, body=%wide.region_3.5_spmd.sunk | while | flops 18874372 | bytes 2290345 | solution.py:27
  523.2 5.2 fusion.8
  528.3 0.6 bitcast_dynamic-update-slice_fusion.2
  529.0 5.2 fusion.8
  534.1 0.6 bitcast_dynamic-update-slice_fusion.2
  534.8 5.2 fusion.8
  540.0 0.6 bitcast_dynamic-update-slice_fusion.2
  540.6 5.2 fusion.8
  545.8 0.6 bitcast_dynamic-update-slice_fusion.2
  546.4 5.2 fusion.8
  551.6 0.6 bitcast_dynamic-update-slice_fusion.2
  552.3 5.2 fusion.8
  557.4 0.6 bitcast_dynamic-update-slice_fusion.2
  558.1 5.2 fusion.8
  563.2 0.6 bitcast_dynamic-update-slice_fusion.2
  563.9 5.2 fusion.8
  569.1 0.6 bitcast_dynamic-update-slice_fusion.2
  569.7 1.7 reshape.40
  571.4 0.0 all-reduce.8.cloned.1.call-update
  571.4 44.5 %all-reduce.8.cloned.1.call-done = f32[32,2048]{1,0:T(8,128)} async-done(((f32[32,2048]{1,0:T(8,128)}), f32[32,2048]{1,0:T(8,128)}) %all-reduce.8.cloned.1.call-update) | async-done | bytes 262160 | tf_op jit(solution)/shard_map/psum | solution.py:53
  615.9 1.7 broadcast_multiply_fusion.1
  (28 shorter events, 0.2 us)
Async XLA Ops:
  6.5 1.9 copy-start
  6.5 5.1 copy-start.3
  6.5 123.6 %reduce-scatter.2.cloned.1.call-start = ((), (), s32[]{:S(2)}) async-start(), calls=%async_computation.1 | async-start | bytes 1081344 | tf_op jit(solution)/shard_map/reduce_scatter | solution.py:44
  11.5 390.2 %all-reduce.4.cloned.1.call-start = ((), (), s32[]{:S(2)}) async-start(), calls=%async_computation.2 | async-start | bytes 4194304 | tf_op jit(solution)/shard_map/psum | solution.py:51
  143.7 258.1 %copy-start.2 = (bf16[32,2048]{1,0:T(8,128)(2,1)S(1)}, bf16[32,2048]{1,0:T(8,128)(2,1)}, u32[]{:S(2)}) copy-start(bf16[32,2048]{1,0:T(8,128)(2,1)} %param.9) | copy-start | bytes 393220
  143.7 258.2 %copy-start.4 = (f32[32]{0:T(128)S(1)}, f32[32]{0:T(128)}, u32[]{:S(2)}) copy-start(f32[32]{0:T(128)} %param.10) | copy-start | bytes 388
  143.7 258.2 %copy-start.1 = (f32[32,256]{1,0:T(8,128)S(1)}, f32[32,256]{1,0:T(8,128)}, u32[]{:S(2)}) copy-start(f32[32,256]{1,0:T(8,128)} %reduce-scatter.2.cloned.1.call-done) | copy-start | bytes 98308
  143.8 379.4 %all-reduce.6.cloned.1.call-start = ((), (), s32[]{:S(2)}) async-start(), calls=%async_computation.3 | async-start | bytes 4194304 | tf_op jit(solution)/shard_map/psum | solution.py:51
  401.8 214.2 %all-reduce.8.cloned.1.call-start = ((), (), s32[]{:S(2)}) async-start(), calls=%async_computation.4 | async-start | bytes 524288 | tf_op jit(solution)/shard_map/psum | solution.py:53
Sparse Core Ops, SparseCore 0:
  11.7 118.4 reduce-scatter.1
  143.9 257.8 all-reduce.3
  404.7 118.3 all-reduce.5
  571.6 44.3 all-reduce.7
